TPU v7x, 512 devices: a whole 4x8x8 slice. The times are simulated.
512 devices in a mesh: leaf: 128 (over y, z, core), sub: 4 (over x).
Axes of the slice: x: 4, y: 8, z: 8, core: 2. Of those that a mesh axis runs over, the one named last changes fastest.
Arguments:
- field: float32 [64, 524288], P(None, ('leaf', 'sub')), may hold values from -6 to 6
- coords: float32 [3, 524288], P(None, ('leaf', 'sub')), may hold values from -6 to 6
- basis: float32 [2048, 64, 256], P(('leaf', 'sub')), may hold values from -0.375 to 0.375
- up_transfer: float32 [2048, 64, 64], P(('leaf', 'sub')), may hold values from -0.1875 to 0.1875
- down_transfer: float32 [2048, 64, 64], P(('leaf', 'sub')), may hold values from -0.75 to 0.75
- couplings: float32 [16384, 64, 64], P(('leaf', 'sub')), may hold values from -0.25 to 0.25
- top_coupling: float32 [128, 128, 64, 64], P('leaf', None, 'sub'), may hold values from -0.25 to 0.25
- send_leaf: int32 [128, 4, 128, 1], P('leaf', 'sub'), may hold values from 0 to 3
- list_slot: int32 [2048, 8], P(('leaf', 'sub')), may hold values from 0 to 127, as said below
- list_block: int32 [2048, 8], P(('leaf', 'sub')), may hold values from 0 to 31
Outputs:
- result: float32 [64, 524288], P(None, ('leaf', 'sub'))
Inputs may be any that keep to these rules, and one draw needn't show every extreme that they name: send_leaf[e, s, d, c] is the leaf, among the 4 of device (e, s), whose skeleton fills slot c of what that device sends to device (d, s). `list_slot`: a list entry q names slot q % 1 from the device q // 1 of the leaf axis with the same sub index; where a device's 4 * 8 list entries are at least 128, every slot is named by some entry of that device, else the device's entries are all different. `list_block`: a list entry names one of the 32 coupling blocks of the leaf's own device.
All inputs are finite; a program needn't handle non-finite values.
Results may differ from a plain program's by a relative error of at most 0.0001.
Values sent between devices are 32-bit elements; how exact they have to be, the bound alone decides.
A program may use at most 64 MiB of HBM per device.

v0:
```python
import math
import jax
import jax.numpy as jnp
from jax import lax
from jax.sharding import PartitionSpec as P

highest = lax.Precision.HIGHEST


def extended(block, sides, width):
    for axis, dim in sides:
        count = lax.axis_size(axis)
        forward = [(i, i + 1) for i in range(count - 1)]
        backward = [(target, source) for source, target in forward]
        low = lax.ppermute(
            lax.slice_in_dim(block, block.shape[dim] - width, None, axis=dim), axis, forward
        )
        high = lax.ppermute(lax.slice_in_dim(block, 0, width, axis=dim), axis, backward)
        block = jnp.concatenate([low, block, high], axis=dim)
    return block


def kernel_block(source_points, target_points, leaf_size):
    dist = jnp.zeros((source_points.shape[1], target_points.shape[1]), jnp.float32)
    for component in range(3):
        gap = source_points[component][:, None] - target_points[component][None, :]
        dist = dist + gap * gap
    return jnp.exp(-0.5 * dist) * (1.0 / math.sqrt(leaf_size))


def add_top(rows, coupling_rows):
    return jnp.einsum("epr,erq->pq", rows, coupling_rows, precision=highest)


def far_terms(incoming, list_slot, chosen, rows, rank):
    gathered = incoming.reshape(-1, rows, rank)[list_slot]
    return jnp.einsum("lkpr,lkrq->lpq", gathered, chosen, precision=highest)


def one_product(
    field,
    coords,
    basis,
    up_transfer,
    down_transfer,
    couplings,
    top_coupling,
    send_leaf,
    list_slot,
    list_block,
):
    rhs_count = field.shape[0]
    leaf_count = basis.shape[0]
    rank = basis.shape[1]
    leaf_size = basis.shape[2]
    stacked = jnp.concatenate([field, coords], 0)
    padded = extended(stacked, ((("leaf", "sub"), 1),), leaf_size)
    leaf_field = field.reshape(rhs_count, leaf_count, leaf_size)
    skeleton = jnp.einsum("pla,lra->lpr", leaf_field, basis, precision=highest)
    outgoing = skeleton[send_leaf.reshape(-1)]
    slot_total = outgoing.shape[0]
    chosen = couplings[list_block]
    incoming = lax.all_to_all(
        outgoing.reshape(slot_total, rhs_count * rank),
        "leaf",
        split_axis=0,
        concat_axis=0,
        tiled=True,
    )
    far = far_terms(incoming, list_slot, chosen, rhs_count, rank)

    def near_leaf(position):
        window = lax.dynamic_slice_in_dim(padded, position * leaf_size, 3 * leaf_size, 1)
        own_points = lax.dynamic_slice_in_dim(
            padded[rhs_count:], (position + 1) * leaf_size, leaf_size, 1
        )
        kernels = kernel_block(window[rhs_count:], own_points, leaf_size)
        return jnp.dot(
            window[:rhs_count], kernels, precision=highest, preferred_element_type=jnp.float32
        )

    near = lax.map(near_leaf, jnp.arange(leaf_count, dtype=jnp.int32))
    parent_part = jnp.einsum("lpr,lrq->pq", skeleton, up_transfer, precision=highest)
    quarter = top_coupling.shape[2]
    coupling_rows = top_coupling[0]
    parent = lax.psum(parent_part, "sub")
    row_start = lax.axis_index("sub") * quarter
    rows = lax.dynamic_slice_in_dim(
        lax.all_gather(parent[None], "leaf", axis=0, tiled=True), row_start, quarter, 2
    )
    top_partial = add_top(rows, coupling_rows)
    top_term = lax.psum(top_partial, "sub")
    coef = far + jnp.einsum("pr,lrq->lpq", top_term, down_transfer, precision=highest)
    total = near + jnp.einsum("lpr,lra->lpa", coef, basis, precision=highest)
    return total.transpose(1, 0, 2).reshape(rhs_count, leaf_count * leaf_size)


def local(
    field,
    coords,
    basis,
    up_transfer,
    down_transfer,
    couplings,
    top_coupling,
    send_leaf,
    list_slot,
    list_block,
):
    current = field
    for repeat in range(2):
        current = one_product(
            current,
            coords,
            basis,
            up_transfer,
            down_transfer,
            couplings,
            top_coupling,
            send_leaf,
            list_slot,
            list_block,
        )
    return current


def solution(mesh):
    in_specs = (
        P(None, ("leaf", "sub")),
        P(None, ("leaf", "sub")),
        P(("leaf", "sub"), None, None),
        P(("leaf", "sub"), None, None),
        P(("leaf", "sub"), None, None),
        P(("leaf", "sub"), None, None),
        P("leaf", None, "sub", None),
        P("leaf", "sub", None, None),
        P(("leaf", "sub"), None),
        P(("leaf", "sub"), None),
    )
    out_specs = P(None, ("leaf", "sub"))
    return jax.shard_map(local, mesh=mesh, in_specs=in_specs, out_specs=out_specs, check_vma=False)
```

profile of v0, /device:TPU:16, one launch (start us, length us, event | category | flops | bytes accessed | tf_op | source)
XLA Modules:
  0.0 379.2 jit_solution(1473924243727374704)
XLA Ops:
  9.2 17.7 %psum.28 = f32[1,64,64]{2,1,0:T(8,128)} all-reduce(f32[1,64,64]{2,1,0:T(8,128)S(1)} %convolution_bitcast_fusion.9), channel_id=1, replica_groups=mesh['leaf'=128,'sub'=4] {'sub'}, use_global_device_ids=true, to_apply=%region_2.3 | all-reduce | flops 4096 | bytes 32768 | tf_op jit(solution)/shard_map/psum | solution.py:86
  28.2 2.8 gather_fusion
  31.0 3.8 copy.27
  34.8 4.1 %copy.28 = f32[128,1,4096]{2,1,0:T(1,128)} copy(f32[128,1,4096]{0,2,1:T(8,128)S(1)} %bitcast.122) | data formatting | bytes 4194304 | tf_op jit(solution)/shard_map/all_to_all | solution.py:63
  38.9 17.8 %all-to-all-start = ((f32[128,1,4096]{2,1,0:T(1,128)}), f32[128,1,4096]{2,1,0:T(1,128)}, u32[]{:S(2)}, u32[]{:S(2)}) async-start(f32[128,1,4096]{2,1,0:T(1,128)} %copy.28), calls=%async_computation | async-start | bytes 4194304 | tf_op jit(solution)/shard_map/all_to_all | solution.py:63
  56.8 1.9 collective-permute-start
  58.8 7.9 %collective-permute-start.1 = (f32[67,256]{1,0:T(8,128)S(1)}, f32[67,256]{1,0:T(8,128)S(1)}, u32[]{:S(2)}, u32[]{:S(2)}) collective-permute-start(f32[67,256]{1,0:T(8,128)S(1)} %get-tuple-element.82), channel_id=1, source_target_pairs={{1,0},{2,1},{3,2},{4,3},{5,4},{6,5},{7,6},{8,7},{9,8},{10,9},{11,1... | collective-permute-start | bytes 205832 | tf_op jit(solution)/shard_map/ppermute | solution.py:18
  68.0 36.9 %collective-permute-done = f32[67,256]{1,0:T(8,128)S(1)} collective-permute-done((f32[67,256]{1,0:T(8,128)S(1)}, f32[67,256]{1,0:T(8,128)S(1)}, u32[]{:S(2)}, u32[]{:S(2)}) %collective-permute-start) | collective-permute-done | bytes 68640 | tf_op jit(solution)/shard_map/ppermute | solution.py:15
  105.0 11.9 %while.20 = (s32[]{:T(128)}, f32[4,64,256]{2,1,0:T(8,128)S(1)}, s32[4]{0:T(128)S(1)}, f32[67,1536]{1,0:T(8,128)S(1)}, s32[]{:T(128)}, /*index=5*/s32[1]{0:T(128)...) while((s32[]{:T(128)}, f32[4,64,256]{2,1,0:T(8,128)S(1)}, ...), condition=%wide.region_1.2_spmd, body=%wide.region_0.1_spmd.sunk | while | flops 152961040 | bytes 339289 | solution.py:82
  117.0 32.6 %all-gather.3.cloned.1.call-done = f32[128,64,64]{2,1,0:T(8,128)} async-done(((f32[1,64,64]{2,1,0:T(8,128)}), f32[128,64,64]{2,1,0:T(8,128)}) %all-gather.3.cloned.1.call-update) | async-done | bytes 2097168 | tf_op jit(solution)/shard_map/all_gather | solution.py:89
  149.6 5.3 %constant_dynamic-slice_fusion.3 = f32[128,64,16]{2,1,0:T(8,128)} fusion(f32[128,64,64]{2,1,0:T(8,128)} %all-gather.3.cloned.1.call-done, s32[]{:T(128)S(6)} %select_n.38), kind=kLoop, calls=%fused_computation.99 | loop fusion | bytes 1048580 | tf_op jit(solution)/shard_map/dynamic_slice | solution.py:88
  154.9 4.0 %copy.41 = f32[128,64,16]{0,1,2:T(8,128)S(1)} copy(f32[128,64,16]{2,1,0:T(8,128)} %constant_dynamic-slice_fusion.3) | data formatting | bytes 1048576
  159.5 17.6 %psum.29 = f32[64,64]{1,0:T(8,128)} all-reduce(f32[64,64]{1,0:T(8,128)S(1)} %convolution_bitcast_fusion.8), channel_id=1, replica_groups=mesh['leaf'=128,'sub'=4] {'sub'}, use_global_device_ids=true, to_apply=%region_3.4 | all-reduce | flops 4096 | bytes 32768 | tf_op jit(solution)/shard_map/psum | solution.py:92
  177.1 5.6 %copy.29 = f32[128,1,4096]{0,2,1:T(8,128)} copy(f32[128,1,4096]{2,1,0:T(1,128)} %all-to-all-done) | data formatting | bytes 4194304 | tf_op jit(solution)/shard_map/all_to_all | solution.py:63
  182.8 5.6 %copy.30 = f32[128,64,64]{2,1,0:T(8,128)} copy(f32[128,64,64]{0,2,1:T(8,128)} %bitcast.123) | data formatting | bytes 4194304 | tf_op jit(solution)/shard_map/reshape | solution.py:36
  188.4 2.9 gather_fusion.1
  196.4 15.0 %psum.30 = f32[1,64,64]{2,1,0:T(8,128)} all-reduce(f32[1,64,64]{2,1,0:T(8,128)S(1)} %convolution_bitcast_fusion.7), channel_id=1, replica_groups=mesh['leaf'=128,'sub'=4] {'sub'}, use_global_device_ids=true, to_apply=%region_6.7 | all-reduce | flops 4096 | bytes 32768 | tf_op jit(solution)/shard_map/psum | solution.py:86
  211.4 2.9 gather_fusion.3
  214.4 4.7 %copy.33 = f32[128,64,64]{0,2,1:T(8,128)} copy(f32[128,64,64]{2,1,0:T(8,128)} %gather_fusion.3) | data formatting | bytes 4194304 | tf_op jit(solution)/shard_map/gather | solution.py:60
  219.1 5.7 %copy.34 = f32[128,1,4096]{2,1,0:T(1,128)} copy(f32[128,1,4096]{0,2,1:T(8,128)} %bitcast.124) | data formatting | bytes 4194304 | tf_op jit(solution)/shard_map/all_to_all | solution.py:63
  224.8 10.4 %all-to-all-start.1 = ((f32[128,1,4096]{2,1,0:T(1,128)}), f32[128,1,4096]{2,1,0:T(1,128)}, u32[]{:S(2)}, u32[]{:S(2)}) async-start(f32[128,1,4096]{2,1,0:T(1,128)} %copy.34), calls=%async_computation.1 | async-start | bytes 4194304 | tf_op jit(solution)/shard_map/all_to_all | solution.py:63
  235.4 2.6 collective-permute-start.2
  238.0 7.2 %collective-permute-start.3 = (f32[67,256]{1,0:T(8,128)S(1)}, f32[67,256]{1,0:T(8,128)S(1)}, u32[]{:S(2)}, u32[]{:S(2)}) collective-permute-start(f32[67,256]{1,0:T(8,128)S(1)} %get-tuple-element.80), channel_id=1, source_target_pairs={{1,0},{2,1},{3,2},{4,3},{5,4},{6,5},{7,6},{8,7},{9,8},{10,9},{11,1... | collective-permute-start | bytes 205832 | tf_op jit(solution)/shard_map/ppermute | solution.py:18
  245.1 40.4 %collective-permute-done.2 = f32[67,256]{1,0:T(8,128)S(1)} collective-permute-done((f32[67,256]{1,0:T(8,128)S(1)}, f32[67,256]{1,0:T(8,128)S(1)}, u32[]{:S(2)}, u32[]{:S(2)}) %collective-permute-start.2) | collective-permute-done | bytes 68640 | tf_op jit(solution)/shard_map/ppermute | solution.py:15
  285.6 11.9 %while.21 = (s32[]{:T(128)}, f32[4,64,256]{2,1,0:T(8,128)S(1)}, s32[4]{0:T(128)S(1)}, f32[67,1536]{1,0:T(8,128)S(1)}, s32[]{:T(128)}, /*index=5*/s32[1]{0:T(128)...) while((s32[]{:T(128)}, f32[4,64,256]{2,1,0:T(8,128)S(1)}, ...), condition=%wide.region_5.6_spmd, body=%wide.region_4.5_spmd.sunk | while | flops 152961040 | bytes 339289 | solution.py:82
  297.6 29.0 %all-gather.5.cloned.1.call-done = f32[128,64,64]{2,1,0:T(8,128)} async-done(((f32[1,64,64]{2,1,0:T(8,128)}), f32[128,64,64]{2,1,0:T(8,128)}) %all-gather.5.cloned.1.call-update) | async-done | bytes 2097168 | tf_op jit(solution)/shard_map/all_gather | solution.py:89
  326.5 5.3 %constant_dynamic-slice_fusion.2 = f32[128,64,16]{2,1,0:T(8,128)} fusion(f32[128,64,64]{2,1,0:T(8,128)} %all-gather.5.cloned.1.call-done, s32[]{:T(128)S(6)} %select_n.38), kind=kLoop, calls=%fused_computation.98 | loop fusion | bytes 1048580 | tf_op jit(solution)/shard_map/dynamic_slice | solution.py:88
  331.8 4.0 %copy.42 = f32[128,64,16]{0,1,2:T(8,128)S(1)} copy(f32[128,64,16]{2,1,0:T(8,128)} %constant_dynamic-slice_fusion.2) | data formatting | bytes 1048576
  336.4 17.6 %psum.31 = f32[64,64]{1,0:T(8,128)} all-reduce(f32[64,64]{1,0:T(8,128)S(1)} %convolution_bitcast_fusion.6), channel_id=1, replica_groups=mesh['leaf'=128,'sub'=4] {'sub'}, use_global_device_ids=true, to_apply=%region_7.8 | all-reduce | flops 4096 | bytes 32768 | tf_op jit(solution)/shard_map/psum | solution.py:92
  354.0 5.6 %copy.35 = f32[128,1,4096]{0,2,1:T(8,128)} copy(f32[128,1,4096]{2,1,0:T(1,128)} %all-to-all-done.1) | data formatting | bytes 4194304 | tf_op jit(solution)/shard_map/all_to_all | solution.py:63
  359.7 5.6 %copy.36 = f32[128,64,64]{2,1,0:T(8,128)} copy(f32[128,64,64]{0,2,1:T(8,128)} %bitcast.125) | data formatting | bytes 4194304 | tf_op jit(solution)/shard_map/reshape | solution.py:36
  365.3 2.8 gather_fusion.4
  (114 shorter events, 29.6 us)
Async XLA Ops:
  6.5 60.9 %copy-start = (f32[32,64,64]{2,1,0:T(8,128)S(1)}, f32[32,64,64]{2,1,0:T(8,128)}, u32[]{:S(2)}) copy-start(f32[32,64,64]{2,1,0:T(8,128)} %param.19) | copy-start | bytes 1572868
  6.5 143.1 %all-gather.3.cloned.1.call-start = ((), (), s32[]{:S(2)}) async-start(), calls=%async_computation.2 | async-start | bytes 4227072 | tf_op jit(solution)/shard_map/all_gather | solution.py:89
  27.6 0.6 copy-start.12
  34.8 22.0 %copy-start.7 = (f32[64,1024]{1,0:T(8,128)S(1)}, f32[64,1024]{1,0:T(8,128)}, u32[]{:S(2)}) copy-start(f32[64,1024]{1,0:T(8,128)} %param.14) | copy-start | bytes 786436
  34.8 22.0 %copy-start.10 = (f32[3,1024]{1,0:T(4,128)S(1)}, f32[3,1024]{1,0:T(4,128)}, u32[]{:S(2)}) copy-start(f32[3,1024]{1,0:T(4,128)} %param.15) | copy-start | bytes 36868
  34.8 31.8 %copy-start.13 = (s32[4,8]{1,0:T(4,128)S(1)}, s32[4,8]{1,0:T(4,128)}, u32[]{:S(2)}) copy-start(s32[4,8]{1,0:T(4,128)} %param.22) | copy-start | bytes 388
  34.8 31.9 %copy-start.14 = (s32[4,8]{1,0:T(4,128)S(1)}, s32[4,8]{1,0:T(4,128)}, u32[]{:S(2)}) copy-start(s32[4,8]{1,0:T(4,128)} %param.23) | copy-start | bytes 388
  38.9 138.2 %all-to-all-start = ((f32[128,1,4096]{2,1,0:T(1,128)}), f32[128,1,4096]{2,1,0:T(1,128)}, u32[]{:S(2)}, u32[]{:S(2)}) async-start(f32[128,1,4096]{2,1,0:T(1,128)} %copy.28), calls=%async_computation | async-start | bytes 4194304 | tf_op jit(solution)/shard_map/all_to_all | solution.py:63
  56.7 269.8 %all-gather.5.cloned.1.call-start = ((), (), s32[]{:S(2)}) async-start(), calls=%async_computation.3 | async-start | bytes 4227072 | tf_op jit(solution)/shard_map/all_gather | solution.py:89
  56.8 48.1 %collective-permute-start = (f32[67,256]{1,0:T(8,128)S(1)}, f32[67,256]{1,0:T(8,128)S(1)}, u32[]{:S(2)}, u32[]{:S(2)}) collective-permute-start(f32[67,256]{1,0:T(8,128)S(1)} %get-tuple-element.81), channel_id=1, source_target_pairs={{0,1},{1,2},{2,3},{3,4},{4,5},{5,6},{6,7},{7,8},{8,9},{9,10},{10,1... | collective-permute-start | bytes 205832 | tf_op jit(solution)/shard_map/ppermute | solution.py:15
  58.8 46.2 %collective-permute-start.1 = (f32[67,256]{1,0:T(8,128)S(1)}, f32[67,256]{1,0:T(8,128)S(1)}, u32[]{:S(2)}, u32[]{:S(2)}) collective-permute-start(f32[67,256]{1,0:T(8,128)S(1)} %get-tuple-element.82), channel_id=1, source_target_pairs={{1,0},{2,1},{3,2},{4,3},{5,4},{6,5},{7,6},{8,7},{9,8},{10,9},{11,1... | collective-permute-start | bytes 205832 | tf_op jit(solution)/shard_map/ppermute | solution.py:18
  117.0 37.9 %copy-start.2 = (f32[4,64,256]{2,1,0:T(8,128)}, f32[4,64,256]{2,1,0:T(8,128)S(1)}, u32[]{:S(2)}) copy-start(f32[4,64,256]{2,1,0:T(8,128)S(1)} %get-tuple-element.49) | copy-start | bytes 786436
  154.9 4.0 %copy-start.4 = (f32[1,128,16,64]{1,3,2,0:T(8,128)S(1)}, f32[1,128,16,64]{1,3,2,0:T(8,128)}, u32[]{:S(2)}) copy-start(f32[1,128,16,64]{1,3,2,0:T(8,128)} %param.20) | copy-start | bytes 1572868
  182.8 9.7 %copy-start.8 = (f32[4,64,64]{2,1,0:T(8,128)S(1)}, f32[4,64,64]{2,1,0:T(8,128)}, u32[]{:S(2)}) copy-start(f32[4,64,64]{2,1,0:T(8,128)} %param.18) | copy-start | bytes 196612
  182.8 10.7 %copy-start.1 = (f32[4,64,256]{2,1,0:T(8,128)S(1)}, f32[4,64,256]{2,1,0:T(8,128)}, u32[]{:S(2)}) copy-start(f32[4,64,256]{2,1,0:T(8,128)} %param.16) | copy-start | bytes 786436
  219.1 16.1 %copy-start.3 = (f32[4,64,256]{2,1,0:T(8,128)S(1)}, f32[4,64,256]{2,1,0:T(8,128)}, u32[]{:S(2)}) copy-start(f32[4,64,256]{2,1,0:T(8,128)} %copy-done.2) | copy-start | bytes 786436
  224.8 129.2 %all-to-all-start.1 = ((f32[128,1,4096]{2,1,0:T(1,128)}), f32[128,1,4096]{2,1,0:T(1,128)}, u32[]{:S(2)}, u32[]{:S(2)}) async-start(f32[128,1,4096]{2,1,0:T(1,128)} %copy.34), calls=%async_computation.1 | async-start | bytes 4194304 | tf_op jit(solution)/shard_map/all_to_all | solution.py:63
  235.4 50.2 %collective-permute-start.2 = (f32[67,256]{1,0:T(8,128)S(1)}, f32[67,256]{1,0:T(8,128)S(1)}, u32[]{:S(2)}, u32[]{:S(2)}) collective-permute-start(f32[67,256]{1,0:T(8,128)S(1)} %get-tuple-element.79), channel_id=1, source_target_pairs={{0,1},{1,2},{2,3},{3,4},{4,5},{5,6},{6,7},{7,8},{8,9},{9,10},{10,1... | collective-permute-start | bytes 205832 | tf_op jit(solution)/shard_map/ppermute | solution.py:15
  238.0 47.6 %collective-permute-start.3 = (f32[67,256]{1,0:T(8,128)S(1)}, f32[67,256]{1,0:T(8,128)S(1)}, u32[]{:S(2)}, u32[]{:S(2)}) collective-permute-start(f32[67,256]{1,0:T(8,128)S(1)} %get-tuple-element.80), channel_id=1, source_target_pairs={{1,0},{2,1},{3,2},{4,3},{5,4},{6,5},{7,6},{8,7},{9,8},{10,9},{11,1... | collective-permute-start | bytes 205832 | tf_op jit(solution)/shard_map/ppermute | solution.py:18
  297.5 29.0 %copy-start.6 = (f32[4,64,256]{2,1,0:T(8,128)}, f32[4,64,256]{2,1,0:T(8,128)S(1)}, u32[]{:S(2)}) copy-start(f32[4,64,256]{2,1,0:T(8,128)S(1)} %get-tuple-element.50) | copy-start | bytes 786436
  331.8 4.0 %copy-start.5 = (f32[1,128,16,64]{1,3,2,0:T(8,128)S(1)}, f32[1,128,16,64]{1,3,2,0:T(8,128)}, u32[]{:S(2)}) copy-start(f32[1,128,16,64]{1,3,2,0:T(8,128)} %param.20) | copy-start | bytes 1572868
  359.7 5.6 %copy-start.11 = (s32[1024]{0:T(1024)S(1)}, s32[1024]{0:T(1024)}, u32[]{:S(2)}) copy-start(s32[1024]{0:T(1024)} %get-tuple-element.84) | copy-start | bytes 12292
  359.7 9.5 %copy-start.9 = (f32[4,64,64]{2,1,0:T(8,128)S(1)}, f32[4,64,64]{2,1,0:T(8,128)}, u32[]{:S(2)}) copy-start(f32[4,64,64]{2,1,0:T(8,128)} %param.18) | copy-start | bytes 196612
Sparse Core Ops, SparseCore 0:
  27.1 122.4 all-gather.2
  211.6 114.9 all-gather.4
where the time goes:
time: 381 us; the launch traced here: 379 us
  waiting for transfers between devices  139 us (36%)
  local copies, waits for them, and re-layouts  79.5 us (21%)
  blocking collectives  67.9 us (18%)
  starting transfers between devices  47.8 us (13%)
  matrix products  18.6 us (5%)
  between operations  13.8 us (4%)
  loops' own time  10.3 us (3%)
    ppermute x2, waiting for transfers between devices, extended(): lax.ppermute(lax.slice_in_dim(block, block.shape[dim] - width, None, axis...  77.3 us
    all_gather x2, waiting for transfers between devices, one_product(): lax.all_gather(parent[None], 'leaf', axis=0, tiled=True)  61.6 us
    psum x2, blocking collectives, one_product(): top_term = lax.psum(top_partial, 'sub')  35.2 us
    psum x2, blocking collectives, one_product(): parent = lax.psum(parent_part, 'sub')  32.7 us
    all_to_all x2, starting transfers between devices, one_product(): lax.all_to_all(outgoing.reshape(slot_total, rhs_count * rank), 'leaf', sp...  28.2 us
    all_to_all x4, local copies, waits for them, and re-layouts, one_product(): lax.all_to_all(outgoing.reshape(slot_total, rhs_count * rank), 'leaf', sp...  21 us
    ppermute x2, starting transfers between devices, extended(): lax.ppermute(lax.slice_in_dim(block, 0, width, axis=dim), axis, backward)  15 us
    gather x4, local copies, waits for them, and re-layouts, one_product(): outgoing = skeleton[send_leaf.reshape(-1)]  14.2 us
  transfers between devices with their start and end apart: 8, of which 4 were waited for; matrix products, arithmetic and copies ran while one was open for 16% of the time, Pallas kernels for 0%

commit v1 on v0

--- a/solution.py
+++ b/solution.py
@@ -89,7 +89,9 @@
         lax.all_gather(parent[None], "leaf", axis=0, tiled=True), row_start, quarter, 2
     )
     top_partial = add_top(rows, coupling_rows)
-    top_term = lax.psum(top_partial, "sub")
+    top_term = top_partial
+    for hop in (1, 2):
+        top_term = top_term + lax.ppermute(top_term, "sub", [(dev, dev ^ hop) for dev in range(4)])
     coef = far + jnp.einsum("pr,lrq->lpq", top_term, down_transfer, precision=highest)
     total = near + jnp.einsum("lpr,lra->lpa", coef, basis, precision=highest)
     return total.transpose(1, 0, 2).reshape(rhs_count, leaf_count * leaf_size)

time: 381 us -> 414 us (1.087)
  the two profiles are of different devices: /device:TPU:16 before, /device:TPU:1 now
where the time goes in v1:
time: 414 us; the launch traced here: 412 us
  waiting for transfers between devices  170 us (41%)
  local copies, waits for them, and re-layouts  93.2 us (23%)
  starting transfers between devices  64.8 us (16%)
  blocking collectives  28.5 us (7%)
  matrix products  24.8 us (6%)
  between operations  13.9 us (3%)
  loops' own time  11 us (3%)
  other arithmetic  5.55 us (1%)
    all_gather x2, waiting for transfers between devices, one_product(): lax.all_gather(parent[None], 'leaf', axis=0, tiled=True)  167 us
    all_to_all x2, starting transfers between devices, one_product(): lax.all_to_all(outgoing.reshape(slot_total, rhs_count * rank), 'leaf', sp...  36.3 us
    psum x2, blocking collectives, one_product(): parent = lax.psum(parent_part, 'sub')  28.5 us
    all_to_all x4, local copies, waits for them, and re-layouts, one_product(): lax.all_to_all(outgoing.reshape(slot_total, rhs_count * rank), 'leaf', sp...  21.2 us
    ppermute x4, starting transfers between devices, one_product(): lax.ppermute(top_term, 'sub', [(dev, dev ^ hop) for dev in range(4)])  15 us
    dot_general x8, matrix products, near_leaf(): jnp.dot(window[:rhs_count], kernels, precision=highest, preferred_element...  14.7 us
    gather x4, local copies, waits for them, and re-layouts, one_product(): outgoing = skeleton[send_leaf.reshape(-1)]  14.3 us
    reshape x2, local copies, waits for them, and re-layouts, far_terms(): gathered = incoming.reshape(-1, rows, rank)[list_slot]  11.3 us
  transfers between devices with their start and end apart: 12, of which 6 were waited for; matrix products, arithmetic and copies ran while one was open for 28% of the time, Pallas kernels for 0%

profile of v1, /device:TPU:1, one launch (start us, length us, event | category | flops | bytes accessed | tf_op | source)
XLA Modules:
  0.0 411.6 jit_solution(12800602765645240326)
XLA Ops:
  9.2 15.1 %psum.14 = f32[1,64,64]{2,1,0:T(8,128)} all-reduce(f32[1,64,64]{2,1,0:T(8,128)S(1)} %convolution_bitcast_fusion.9), channel_id=1, replica_groups=mesh['leaf'=128,'sub'=4] {'sub'}, use_global_device_ids=true, to_apply=%region_2.3 | all-reduce | flops 4096 | bytes 32768 | tf_op jit(solution)/shard_map/psum | solution.py:86
  25.6 2.8 gather_fusion
  28.4 3.8 copy.31
  32.2 4.1 copy.32
  36.3 21.5 %all-to-all-start = ((f32[128,1,4096]{2,1,0:T(1,128)}), f32[128,1,4096]{2,1,0:T(1,128)}, u32[]{:S(2)}, u32[]{:S(2)}) async-start(f32[128,1,4096]{2,1,0:T(1,128)} %copy.32), calls=%async_computation | async-start | bytes 4194304 | tf_op jit(solution)/shard_map/all_to_all | solution.py:63
  57.9 1.9 collective-permute-start
  59.8 4.9 %collective-permute-start.1 = (f32[67,256]{1,0:T(8,128)S(1)}, f32[67,256]{1,0:T(8,128)S(1)}, u32[]{:S(2)}, u32[]{:S(2)}) collective-permute-start(f32[67,256]{1,0:T(8,128)S(1)} %get-tuple-element.82), channel_id=1, source_target_pairs={{1,0},{2,1},{3,2},{4,3},{5,4},{6,5},{7,6},{8,7},{9,8},{10,9},{11,1... | collective-permute-start | bytes 205832 | tf_op jit(solution)/shard_map/ppermute | solution.py:18
  67.0 84.4 %all-gather.3.cloned.1.call-done = f32[128,64,64]{2,1,0:T(8,128)} async-done(((f32[1,64,64]{2,1,0:T(8,128)}), f32[128,64,64]{2,1,0:T(8,128)}) %all-gather.3.cloned.1.call-update) | async-done | bytes 2097168 | tf_op jit(solution)/shard_map/all_gather | solution.py:89
  151.3 5.3 %constant_dynamic-slice_fusion.3 = f32[128,64,16]{2,1,0:T(8,128)} fusion(f32[128,64,64]{2,1,0:T(8,128)} %all-gather.3.cloned.1.call-done, s32[]{:T(128)S(6)} %select_n.38), kind=kLoop, calls=%fused_computation.101 | loop fusion | bytes 1048580 | tf_op jit(solution)/shard_map/dynamic_slice | solution.py:88
  156.7 4.0 copy.45
  161.9 3.1 collective-permute-start.2
  165.0 22.3 %while.20 = (s32[]{:T(128)}, f32[4,64,256]{2,1,0:T(8,128)S(1)}, s32[4]{0:T(128)S(1)}, f32[67,1536]{1,0:T(8,128)}, s32[]{:T(128)}, /*index=5*/s32[1]{0:T(128)}, s...) while((s32[]{:T(128)}, f32[4,64,256]{2,1,0:T(8,128)S(1)}, s32[4]{0:T(128)S(1)}, ...), condition=%wide.region_1.2_spmd, body=%wide.region_0.1_spmd.sunk | while | flops 152961040 | bytes 339797 | solution.py:82
  187.4 5.7 %copy.33 = f32[128,1,4096]{0,2,1:T(8,128)} copy(f32[128,1,4096]{2,1,0:T(1,128)} %all-to-all-done) | data formatting | bytes 4194304 | tf_op jit(solution)/shard_map/all_to_all | solution.py:63
  193.1 5.6 %copy.34 = f32[128,64,64]{2,1,0:T(8,128)} copy(f32[128,64,64]{0,2,1:T(8,128)} %bitcast.123) | data formatting | bytes 4194304 | tf_op jit(solution)/shard_map/reshape | solution.py:36
  198.7 2.9 gather_fusion.1
  202.5 4.5 %collective-permute-start.3 = (f32[64,64]{1,0:T(8,128)S(1)}, f32[64,64]{1,0:T(8,128)S(1)}, u32[]{:S(2)}, u32[]{:S(2)}) collective-permute-start(f32[64,64]{1,0:T(8,128)S(1)} %add.93), channel_id=1, source_target_pairs={{0,2},{1,3},{2,0},{3,1},{4,6},{5,7},{6,4},{7,5},{8,10},{9,11},{10,... | collective-permute-start | bytes 49160 | tf_op jit(solution)/shard_map/ppermute | solution.py:94
  211.0 13.4 %psum.15 = f32[1,64,64]{2,1,0:T(8,128)} all-reduce(f32[1,64,64]{2,1,0:T(8,128)S(1)} %convolution_bitcast_fusion.7), channel_id=1, replica_groups=mesh['leaf'=128,'sub'=4] {'sub'}, use_global_device_ids=true, to_apply=%region_5.6 | all-reduce | flops 4096 | bytes 32768 | tf_op jit(solution)/shard_map/psum | solution.py:86
  224.4 2.9 gather_fusion.3
  227.3 4.8 %copy.37 = f32[128,64,64]{0,2,1:T(8,128)} copy(f32[128,64,64]{2,1,0:T(8,128)} %gather_fusion.3) | data formatting | bytes 4194304 | tf_op jit(solution)/shard_map/gather | solution.py:60
  232.1 5.7 %copy.38 = f32[128,1,4096]{2,1,0:T(1,128)} copy(f32[128,1,4096]{0,2,1:T(8,128)} %bitcast.124) | data formatting | bytes 4194304 | tf_op jit(solution)/shard_map/all_to_all | solution.py:63
  237.8 14.8 %all-to-all-start.1 = ((f32[128,1,4096]{2,1,0:T(1,128)}), f32[128,1,4096]{2,1,0:T(1,128)}, u32[]{:S(2)}, u32[]{:S(2)}) async-start(f32[128,1,4096]{2,1,0:T(1,128)} %copy.38), calls=%async_computation.1 | async-start | bytes 4194304 | tf_op jit(solution)/shard_map/all_to_all | solution.py:63
  252.8 1.9 collective-permute-start.4
  254.7 4.9 %collective-permute-start.5 = (f32[67,256]{1,0:T(8,128)S(1)}, f32[67,256]{1,0:T(8,128)S(1)}, u32[]{:S(2)}, u32[]{:S(2)}) collective-permute-start(f32[67,256]{1,0:T(8,128)S(1)} %get-tuple-element.80), channel_id=1, source_target_pairs={{1,0},{2,1},{3,2},{4,3},{5,4},{6,5},{7,6},{8,7},{9,8},{10,9},{11,1... | collective-permute-start | bytes 205832 | tf_op jit(solution)/shard_map/ppermute | solution.py:18
  261.8 82.7 %all-gather.5.cloned.1.call-done = f32[128,64,64]{2,1,0:T(8,128)} async-done(((f32[1,64,64]{2,1,0:T(8,128)}), f32[128,64,64]{2,1,0:T(8,128)}) %all-gather.5.cloned.1.call-update) | async-done | bytes 2097168 | tf_op jit(solution)/shard_map/all_gather | solution.py:89
  344.5 5.3 %constant_dynamic-slice_fusion.2 = f32[128,64,16]{2,1,0:T(8,128)} fusion(f32[128,64,64]{2,1,0:T(8,128)} %all-gather.5.cloned.1.call-done, s32[]{:T(128)S(6)} %select_n.38), kind=kLoop, calls=%fused_computation.100 | loop fusion | bytes 1048580 | tf_op jit(solution)/shard_map/dynamic_slice | solution.py:88
  349.8 4.0 copy.46
  355.0 3.1 collective-permute-start.6
  358.2 23.0 %while.21 = (s32[]{:T(128)}, f32[4,64,256]{2,1,0:T(8,128)S(1)}, s32[4]{0:T(128)S(1)}, f32[67,1536]{1,0:T(8,128)}, s32[]{:T(128)}, /*index=5*/s32[1]{0:T(128)}, s...) while((s32[]{:T(128)}, f32[4,64,256]{2,1,0:T(8,128)S(1)}, s32[4]{0:T(128)S(1)}, ...), condition=%wide.region_4.5_spmd, body=%wide.region_3.4_spmd.sunk | while | flops 152961040 | bytes 339797 | solution.py:82
  381.2 5.7 %copy.39 = f32[128,1,4096]{0,2,1:T(8,128)} copy(f32[128,1,4096]{2,1,0:T(1,128)} %all-to-all-done.1) | data formatting | bytes 4194304 | tf_op jit(solution)/shard_map/all_to_all | solution.py:63
  387.0 5.6 %copy.40 = f32[128,64,64]{2,1,0:T(8,128)} copy(f32[128,64,64]{0,2,1:T(8,128)} %bitcast.125) | data formatting | bytes 4194304 | tf_op jit(solution)/shard_map/reshape | solution.py:36
  392.6 2.8 gather_fusion.4
  396.2 4.3 %collective-permute-start.7 = (f32[64,64]{1,0:T(8,128)S(1)}, f32[64,64]{1,0:T(8,128)S(1)}, u32[]{:S(2)}, u32[]{:S(2)}) collective-permute-start(f32[64,64]{1,0:T(8,128)S(1)} %add.97), channel_id=1, source_target_pairs={{0,2},{1,3},{2,0},{3,1},{4,6},{5,7},{6,4},{7,5},{8,10},{9,11},{10,... | collective-permute-start | bytes 49160 | tf_op jit(solution)/shard_map/ppermute | solution.py:94
  (124 shorter events, 55.1 us)
Async XLA Ops:
  6.5 59.0 %copy-start = (f32[32,64,64]{2,1,0:T(8,128)S(1)}, f32[32,64,64]{2,1,0:T(8,128)}, u32[]{:S(2)}) copy-start(f32[32,64,64]{2,1,0:T(8,128)} %param.19) | copy-start | bytes 1572868
  6.5 144.8 %all-gather.3.cloned.1.call-start = ((), (), s32[]{:S(2)}) async-start(), calls=%async_computation.2 | async-start | bytes 4227072 | tf_op jit(solution)/shard_map/all_gather | solution.py:89
  25.0 0.6 copy-start.13
  32.2 25.6 %copy-start.7 = (f32[64,1024]{1,0:T(8,128)S(1)}, f32[64,1024]{1,0:T(8,128)}, u32[]{:S(2)}) copy-start(f32[64,1024]{1,0:T(8,128)} %param.14) | copy-start | bytes 786436
  32.2 25.7 %copy-start.11 = (f32[3,1024]{1,0:T(4,128)S(1)}, f32[3,1024]{1,0:T(4,128)}, u32[]{:S(2)}) copy-start(f32[3,1024]{1,0:T(4,128)} %param.15) | copy-start | bytes 36868
  32.2 32.5 %copy-start.14 = (s32[4,8]{1,0:T(4,128)S(1)}, s32[4,8]{1,0:T(4,128)}, u32[]{:S(2)}) copy-start(s32[4,8]{1,0:T(4,128)} %param.22) | copy-start | bytes 388
  32.2 32.6 %copy-start.15 = (s32[4,8]{1,0:T(4,128)S(1)}, s32[4,8]{1,0:T(4,128)}, u32[]{:S(2)}) copy-start(s32[4,8]{1,0:T(4,128)} %param.23) | copy-start | bytes 388
  36.3 151.0 %all-to-all-start = ((f32[128,1,4096]{2,1,0:T(1,128)}), f32[128,1,4096]{2,1,0:T(1,128)}, u32[]{:S(2)}, u32[]{:S(2)}) async-start(f32[128,1,4096]{2,1,0:T(1,128)} %copy.32), calls=%async_computation | async-start | bytes 4194304 | tf_op jit(solution)/shard_map/all_to_all | solution.py:63
  57.8 286.7 %all-gather.5.cloned.1.call-start = ((), (), s32[]{:S(2)}) async-start(), calls=%async_computation.3 | async-start | bytes 4227072 | tf_op jit(solution)/shard_map/all_gather | solution.py:89
  57.9 8.2 %collective-permute-start = (f32[67,256]{1,0:T(8,128)S(1)}, f32[67,256]{1,0:T(8,128)S(1)}, u32[]{:S(2)}, u32[]{:S(2)}) collective-permute-start(f32[67,256]{1,0:T(8,128)S(1)} %get-tuple-element.81), channel_id=1, source_target_pairs={{0,1},{1,2},{2,3},{3,4},{4,5},{5,6},{6,7},{7,8},{8,9},{9,10},{10,1... | collective-permute-start | bytes 205832 | tf_op jit(solution)/shard_map/ppermute | solution.py:15
  59.8 6.3 %collective-permute-start.1 = (f32[67,256]{1,0:T(8,128)S(1)}, f32[67,256]{1,0:T(8,128)S(1)}, u32[]{:S(2)}, u32[]{:S(2)}) collective-permute-start(f32[67,256]{1,0:T(8,128)S(1)} %get-tuple-element.82), channel_id=1, source_target_pairs={{1,0},{2,1},{3,2},{4,3},{5,4},{6,5},{7,6},{8,7},{9,8},{10,9},{11,1... | collective-permute-start | bytes 205832 | tf_op jit(solution)/shard_map/ppermute | solution.py:18
  156.7 4.0 copy-start.4
  161.9 39.8 %collective-permute-start.2 = (f32[64,64]{1,0:T(8,128)}, f32[64,64]{1,0:T(8,128)}, u32[]{:S(2)}, u32[]{:S(2)}) collective-permute-start(f32[64,64]{1,0:T(8,128)} %convolution_bitcast_fusion.8), channel_id=1, source_target_pairs={{0,1},{1,0},{2,3},{3,2},{4,5},{5,4},{6,7},{7,6},{8,9},{9,8},{10,11... | collective-permute-start | bytes 49160 | tf_op jit(solution)/shard_map/ppermute | solution.py:94
  187.3 11.4 %copy-start.2 = (f32[4,64,256]{2,1,0:T(8,128)}, f32[4,64,256]{2,1,0:T(8,128)S(1)}, u32[]{:S(2)}) copy-start(f32[4,64,256]{2,1,0:T(8,128)S(1)} %get-tuple-element.49) | copy-start | bytes 786436
  193.1 15.6 %copy-start.8 = (f32[4,64,64]{2,1,0:T(8,128)S(1)}, f32[4,64,64]{2,1,0:T(8,128)}, u32[]{:S(2)}) copy-start(f32[4,64,64]{2,1,0:T(8,128)} %param.18) | copy-start | bytes 196612
  193.1 15.9 %copy-start.1 = (f32[4,64,256]{2,1,0:T(8,128)S(1)}, f32[4,64,256]{2,1,0:T(8,128)}, u32[]{:S(2)}) copy-start(f32[4,64,256]{2,1,0:T(8,128)} %param.16) | copy-start | bytes 786436
  201.7 9.0 %copy-start.10 = (f32[4,64,64]{2,1,0:T(8,128)S(1)}, f32[4,64,64]{2,1,0:T(8,128)}, u32[]{:S(2)}) copy-start(f32[4,64,64]{2,1,0:T(8,128)} %param.17) | copy-start | bytes 196612
  202.5 6.2 %collective-permute-start.3 = (f32[64,64]{1,0:T(8,128)S(1)}, f32[64,64]{1,0:T(8,128)S(1)}, u32[]{:S(2)}, u32[]{:S(2)}) collective-permute-start(f32[64,64]{1,0:T(8,128)S(1)} %add.93), channel_id=1, source_target_pairs={{0,2},{1,3},{2,0},{3,1},{4,6},{5,7},{6,4},{7,5},{8,10},{9,11},{10,... | collective-permute-start | bytes 49160 | tf_op jit(solution)/shard_map/ppermute | solution.py:94
  232.1 20.5 %copy-start.3 = (f32[4,64,256]{2,1,0:T(8,128)S(1)}, f32[4,64,256]{2,1,0:T(8,128)}, u32[]{:S(2)}) copy-start(f32[4,64,256]{2,1,0:T(8,128)} %copy-done.2) | copy-start | bytes 786436
  237.8 143.4 %all-to-all-start.1 = ((f32[128,1,4096]{2,1,0:T(1,128)}), f32[128,1,4096]{2,1,0:T(1,128)}, u32[]{:S(2)}, u32[]{:S(2)}) async-start(f32[128,1,4096]{2,1,0:T(1,128)} %copy.38), calls=%async_computation.1 | async-start | bytes 4194304 | tf_op jit(solution)/shard_map/all_to_all | solution.py:63
  252.8 7.3 %collective-permute-start.4 = (f32[67,256]{1,0:T(8,128)S(1)}, f32[67,256]{1,0:T(8,128)S(1)}, u32[]{:S(2)}, u32[]{:S(2)}) collective-permute-start(f32[67,256]{1,0:T(8,128)S(1)} %get-tuple-element.79), channel_id=1, source_target_pairs={{0,1},{1,2},{2,3},{3,4},{4,5},{5,6},{6,7},{7,8},{8,9},{9,10},{10,1... | collective-permute-start | bytes 205832 | tf_op jit(solution)/shard_map/ppermute | solution.py:15
  254.7 6.2 %collective-permute-start.5 = (f32[67,256]{1,0:T(8,128)S(1)}, f32[67,256]{1,0:T(8,128)S(1)}, u32[]{:S(2)}, u32[]{:S(2)}) collective-permute-start(f32[67,256]{1,0:T(8,128)S(1)} %get-tuple-element.80), channel_id=1, source_target_pairs={{1,0},{2,1},{3,2},{4,3},{5,4},{6,5},{7,6},{8,7},{9,8},{10,9},{11,1... | collective-permute-start | bytes 205832 | tf_op jit(solution)/shard_map/ppermute | solution.py:18
  349.8 4.0 copy-start.5
  355.0 40.4 %collective-permute-start.6 = (f32[64,64]{1,0:T(8,128)}, f32[64,64]{1,0:T(8,128)}, u32[]{:S(2)}, u32[]{:S(2)}) collective-permute-start(f32[64,64]{1,0:T(8,128)} %convolution_bitcast_fusion.6), channel_id=1, source_target_pairs={{0,1},{1,0},{2,3},{3,2},{4,5},{5,4},{6,7},{7,6},{8,9},{9,8},{10,11... | collective-permute-start | bytes 49160 | tf_op jit(solution)/shard_map/ppermute | solution.py:94
  381.2 5.8 %copy-start.6 = (f32[4,64,256]{2,1,0:T(8,128)}, f32[4,64,256]{2,1,0:T(8,128)S(1)}, u32[]{:S(2)}) copy-start(f32[4,64,256]{2,1,0:T(8,128)S(1)} %get-tuple-element.50) | copy-start | bytes 786436
  387.0 5.6 %copy-start.12 = (s32[1024]{0:T(1024)S(1)}, s32[1024]{0:T(1024)}, u32[]{:S(2)}) copy-start(s32[1024]{0:T(1024)} %get-tuple-element.84) | copy-start | bytes 12292
  387.0 15.4 %copy-start.9 = (f32[4,64,64]{2,1,0:T(8,128)S(1)}, f32[4,64,64]{2,1,0:T(8,128)}, u32[]{:S(2)}) copy-start(f32[4,64,64]{2,1,0:T(8,128)} %param.18) | copy-start | bytes 196612
  396.2 6.2 %collective-permute-start.7 = (f32[64,64]{1,0:T(8,128)S(1)}, f32[64,64]{1,0:T(8,128)S(1)}, u32[]{:S(2)}, u32[]{:S(2)}) collective-permute-start(f32[64,64]{1,0:T(8,128)S(1)} %add.97), channel_id=1, source_target_pairs={{0,2},{1,3},{2,0},{3,1},{4,6},{5,7},{6,4},{7,5},{8,10},{9,11},{10,... | collective-permute-start | bytes 49160 | tf_op jit(solution)/shard_map/ppermute | solution.py:94
Sparse Core Ops, SparseCore 0:
  24.5 126.8 all-gather.2
  224.5 119.9 all-gather.4
